TPU v7x, 512 devices: a whole 4x4x16 slice. The times are simulated.
512 devices in a mesh: lat: 16 (over z_hi, y), lon: 32 (over z_lo, x, core).
Axes of the slice: x: 4, y: 4, z: 16 (z_hi: 4, z_lo: 4; z = z_hi * 4 + z_lo), core: 2. Of those that a mesh axis runs over, the one named last changes fastest.
Arguments:
- queries: float32 [64, 1024, 512], P('lat', 'lon'), may hold values from -80 to 80
- key_rows: float32 [512, 512], P(('lat', 'lon')), may hold values from -8 to 8
- value_rows: float32 [512, 512], P(('lat', 'lon')), may hold values from -6 to 6
- cotangent: float32 [64, 1024, 512], P('lat', 'lon'), may hold values from -25 to 25
- conv_taps: float32 [9, 512], replicated, may hold values from -1.75 to 1.75
Outputs:
- query_grad: float32 [64, 1024, 512], P('lat', 'lon')
- key_grad: float32 [512, 512], P(('lat', 'lon'))
- value_grad: float32 [512, 512], P(('lat', 'lon'))
- tap_update: float32 [9, 512], replicated
All inputs are finite; a program needn't handle non-finite values.
Results may differ from a plain program's by a relative error of at most 0.0003.
Values sent between devices are 32-bit elements; how exact they have to be, the bound alone decides.
A program may use at most 64 MiB of HBM per device.

v0:
```python
import jax
import jax.numpy as jnp
from jax import lax
from jax.sharding import PartitionSpec as P

HD = 64
HIGH = lax.Precision.HIGHEST
OFFSETS = ((-1, -1), (-1, 0), (-1, 1), (0, -1), (0, 0), (0, 1), (1, -1), (1, 0), (1, 1))


def joined_along(pieces, dim):
    lengths = list(pieces.shape[1:])
    lengths[dim] *= pieces.shape[0]
    return jnp.moveaxis(pieces, 0, dim).reshape(lengths)


def copy_for_each(value, axis):
    copies = jnp.broadcast_to(value, (lax.axis_size(axis), *value.shape))
    return lax.all_to_all(copies, axis, split_axis=0, concat_axis=0, tiled=True)


def gather_directly(value, axis, dim):
    return joined_along(copy_for_each(value, axis), dim)


def extended(value, sides, width):
    for axis, dim in sides:
        peers, length = (lax.axis_size(axis), value.shape[dim])
        up = [(i, (i + 1) % peers) for i in range(peers)]
        down = [(j, i) for i, j in up]
        last = lax.slice_in_dim(value, length - width, length, axis=dim)
        initial = lax.slice_in_dim(value, 0, width, axis=dim)
        before = lax.ppermute(last, axis, up)
        after = lax.ppermute(initial, axis, down)
        value = jnp.concatenate([before, value, after], axis=dim)
    return value


def cut_along(value, dim, peers):
    lengths = value.shape
    pieces = value.reshape(*lengths[:dim], peers, lengths[dim] // peers, *lengths[dim + 1 :])
    return jnp.moveaxis(pieces, dim, 0)


def summed_on_arrival(value, axis, dim):
    peers = lax.axis_size(axis)
    pieces = lax.all_to_all(cut_along(value, dim, peers), axis, 0, 0, tiled=True)
    return jnp.sum(pieces, axis=0)


def split_heads(matrix):
    return matrix.reshape(matrix.shape[0], -1, HD)


def latitude_weights(row_count, band_index, band_count):
    line_total = row_count * band_count
    centres = (jnp.arange(line_total, dtype=jnp.float32) + 0.5) * (jnp.pi / line_total)
    mean_cosine = jnp.sum(jnp.sin(centres)) / line_total
    mine = (band_index * row_count + jnp.arange(row_count, dtype=jnp.int32)).astype(jnp.float32)
    return jnp.sin((mine + 0.5) * (jnp.pi / line_total)) / mean_cosine


def close_poles(padded, row_dim, band_index, band_count):
    height = padded.shape[row_dim]
    positions = jnp.arange(height)
    outside = (positions == 0) & (band_index == 0) | (positions == height - 1) & (
        band_index == band_count - 1
    )
    shape_mask = [1] * padded.ndim
    shape_mask[row_dim] = height
    return jnp.where(outside.reshape(shape_mask), 0.0, padded)


def spread_taps(weighted, grad_padded, conv_taps):
    row_count, col_count = (weighted.shape[0], weighted.shape[1])
    result = weighted
    for tap_index, (shift_row, shift_col) in enumerate(OFFSETS):
        result = (
            result
            + conv_taps[tap_index]
            * grad_padded[
                1 - shift_row : 1 - shift_row + row_count, 1 - shift_col : 1 - shift_col + col_count
            ]
        )
    return result


def tap_terms(weighted, out_padded):
    row_count, col_count = (weighted.shape[0], weighted.shape[1])
    term_list = []
    for shift_row, shift_col in OFFSETS:
        term_list.append(
            jnp.sum(
                out_padded[
                    1 + shift_row : 1 + shift_row + row_count,
                    1 + shift_col : 1 + shift_col + col_count,
                ]
                * weighted,
                axis=(0, 1),
            )
        )
    return jnp.stack(term_list)


def group_logits(query_part, key_part):
    return jnp.einsum(
        "qhd,khd->hqk", split_heads(query_part), split_heads(key_part), precision=HIGH
    ) * HD ** (-0.5)


def body(queries, key_rows, value_rows, cotangent, conv_taps):
    row_count, col_count, channels = queries.shape
    band_count = lax.axis_size("lat")
    band_index = lax.axis_index("lat")
    weighted = cotangent * latitude_weights(row_count, band_index, band_count)[:, None, None]
    paired_rows = jnp.concatenate([key_rows, value_rows], 1)
    paired_sector = gather_directly(paired_rows, "lon", 0)
    paired_all = lax.all_gather(paired_sector, "lat", axis=0, tiled=True)
    key_all = paired_all[:, :channels]
    value_all = paired_all[:, channels:]
    token_count = row_count * col_count
    key_count = key_all.shape[0]
    query_flat = queries.reshape(token_count, channels)
    group_width = 2 * HD
    group_count = channels // group_width
    outputs = []
    peaks = []
    sums_soft = []
    for group_index in range(group_count):
        col_start = group_index * group_width
        col_stop = col_start + group_width
        logits = group_logits(query_flat[:, col_start:col_stop], key_all[:, col_start:col_stop])
        row_peak = jnp.max(logits, -1, keepdims=True)
        raised = jnp.exp(logits - row_peak)
        normaliser = jnp.sum(raised, -1, keepdims=True)
        soft_weights = raised / normaliser
        outputs.append(
            jnp.einsum(
                "hqk,khd->qhd",
                soft_weights,
                split_heads(value_all[:, col_start:col_stop]),
                precision=HIGH,
            ).reshape(token_count, group_width)
        )
        peaks.append(row_peak)
        sums_soft.append(normaliser)
    out_flat = jnp.concatenate(outputs, 1)
    out_grid = out_flat.reshape(row_count, col_count, channels)
    both_padded = close_poles(
        extended(jnp.stack([weighted, out_grid]), (("lat", 1), ("lon", 2)), 1),
        1,
        band_index,
        band_count,
    )
    grad_padded = both_padded[0]
    out_padded = both_padded[1]
    out_grad = spread_taps(weighted, grad_padded, conv_taps)
    tap_sum = lax.psum(tap_terms(weighted, out_padded), ("lat", "lon"))
    tap_update = tap_sum / jnp.sqrt(jnp.mean(tap_sum * tap_sum) + 1e-06)
    grad_flat = out_grad.reshape(token_count, channels)
    query_parts = []
    key_parts = []
    value_parts = []
    for group_index in range(group_count):
        col_start = group_index * group_width
        col_stop = col_start + group_width
        query_heads = split_heads(query_flat[:, col_start:col_stop])
        key_heads = split_heads(key_all[:, col_start:col_stop])
        logits = jnp.einsum("qhd,khd->hqk", query_heads, key_heads, precision=HIGH) * HD ** (-0.5)
        soft_weights = jnp.exp(logits - peaks[group_index]) / sums_soft[group_index]
        grad_heads = split_heads(grad_flat[:, col_start:col_stop])
        value_parts.append(
            jnp.einsum("hqk,qhd->khd", soft_weights, grad_heads, precision=HIGH).reshape(
                key_count, group_width
            )
        )
        prob_grad = jnp.einsum(
            "qhd,khd->hqk",
            grad_heads,
            split_heads(value_all[:, col_start:col_stop]),
            precision=HIGH,
        )
        row_dot = jnp.transpose(
            jnp.sum(grad_heads * split_heads(out_flat[:, col_start:col_stop]), -1)
        )[:, :, None]
        logit_grad = soft_weights * (prob_grad - row_dot)
        query_parts.append(
            (
                jnp.einsum("hqk,khd->qhd", logit_grad, key_heads, precision=HIGH) * HD ** (-0.5)
            ).reshape(token_count, group_width)
        )
        key_parts.append(
            (
                jnp.einsum("hqk,qhd->khd", logit_grad, query_heads, precision=HIGH) * HD ** (-0.5)
            ).reshape(key_count, group_width)
        )
    paired_terms = jnp.concatenate(key_parts + value_parts, 1)
    paired_band = lax.psum_scatter(paired_terms, "lat", scatter_dimension=0, tiled=True)
    paired_grad = summed_on_arrival(paired_band, "lon", 0)
    key_grad = paired_grad[:, :channels]
    value_grad = paired_grad[:, channels:]
    query_grad = jnp.concatenate(query_parts, 1).reshape(row_count, col_count, channels)
    return (query_grad, key_grad, value_grad, tap_update)


def solution(mesh):
    placed = (
        P("lat", "lon", None),
        P(("lat", "lon"), None),
        P(("lat", "lon"), None),
        P("lat", "lon", None),
        P(),
    )
    return jax.shard_map(
        body,
        mesh=mesh,
        in_specs=placed,
        out_specs=(P("lat", "lon", None), P(("lat", "lon"), None), P(("lat", "lon"), None), P()),
        check_vma=False,
    )
```

profile of v0, /device:TPU:1, one launch (start us, length us, event | category | flops | bytes accessed | tf_op | source)
XLA Modules:
  0.0 343.2 jit_solution(12765066276765064027)
XLA Ops:
  8.0 18.8 %all_to_all.10 = f32[32,1,1024]{2,1,0:T(1,128)} all-to-all(f32[32,1,1024]{2,1,0:T(1,128)S(1)} %broadcast_in_dim.10), channel_id=1, replica_groups=mesh['lat'=16,'lon'=32] {'lon'}, dimensions={0} | all-to-all | bytes 262144 | tf_op jit(solution)/shard_map/all_to_all | solution.py:19
  30.8 1.0 fusion.50
  31.8 88.1 %all-gather.3.cloned.1.call-done = f32[512,1,1024]{2,1,0:T(1,128)} async-done(((f32[32,1,1024]{2,1,0:T(1,128)}), f32[512,1,1024]{2,1,0:T(1,128)}) %all-gather.3.cloned.1.call-update) | async-done | bytes 2097168 | tf_op jit(solution)/shard_map/all_gather | solution.py:118
  120.0 2.1 copy.158
  126.7 1.0 fusion.58
  127.8 1.1 convolution_bitcast_fusion.2
  133.1 1.4 convolution_bitcast_fusion.3
  134.8 2.1 collective-permute-start
  136.9 9.2 %collective-permute-start.1 = (f32[2,1,32,512]{3,2,1,0:T(8,128)S(1)}, f32[2,1,32,512]{3,2,1,0:T(8,128)S(1)}, u32[]{:S(2)}, u32[]{:S(2)}) collective-permute-start(f32[2,1,32,512]{3,2,1,0:T(8,128)S(1)} %get-tuple-element.26), channel_id=1, source_target_pairs={{32,0},{64,32},{96,64},{128,96},{160,128},{192,160},{224,192},{256... | collective-permute-start | bytes 393224 | tf_op jit(solution)/shard_map/ppermute | solution.py:34
  146.1 4.7 %collective-permute-done = f32[2,1,32,512]{3,2,1,0:T(8,128)S(1)} collective-permute-done((f32[2,1,32,512]{3,2,1,0:T(8,128)S(1)}, f32[2,1,32,512]{3,2,1,0:T(8,128)S(1)}, u32[]{:S(2)}, u32[]{:S(2)}) %collective-permute-start) | collective-permute-done | bytes 131104 | tf_op jit(solution)/shard_map/ppermute | solution.py:33
  150.9 3.2 collective-permute-start.2
  154.1 2.1 collective-permute-start.3
  156.3 3.3 collective-permute-done.3
  160.9 1.6 copy.153
  163.3 1.6 copy.155
  165.8 1.6 copy.154
  168.2 1.6 copy.156
  170.8 1.6 fusion.38
  181.8 1.9 copy.146
  184.1 117.4 %psum.7 = f32[9,512]{1,0:T(8,128)S(1)} all-reduce(f32[9,512]{1,0:T(8,128)S(1)} %stack.47), channel_id=1, replica_groups=mesh['lat'=16,'lon'=32] {'lat','lon'}, use_global_device_ids=true, to_apply=%region_24.25 | all-reduce | flops 4608 | bytes 36864 | tf_op jit(solution)/shard_map/psum | solution.py:158
  304.9 13.6 %reduce-scatter.4.cloned.1.call-done = f32[32,1024]{1,0:T(8,128)} async-done(((f32[512,1024]{1,0:T(8,128)}), f32[32,1024]{1,0:T(8,128)}) %reduce-scatter.4.cloned.1.call-update) | async-done | bytes 131088
  318.5 1.1 copy.147
  320.4 6.7 %all-to-all-start.1 = ((f32[32,1,1024]{2,1,0:T(1,128)}), f32[32,1,1024]{2,1,0:T(1,128)S(1)}, u32[]{:S(2)}, u32[]{:S(2)}) async-start(f32[32,1,1024]{2,1,0:T(1,128)} %copy.125), calls=%async_computation.1 | async-start | bytes 262144 | tf_op jit(solution)/shard_map/all_to_all | solution.py:47
  329.2 6.5 %all-to-all-done.1 = f32[32,1,1024]{2,1,0:T(1,128)S(1)} async-done(((f32[32,1,1024]{2,1,0:T(1,128)}), f32[32,1,1024]{2,1,0:T(1,128)S(1)}, u32[]{:S(2)}, u32[]{:S(2)}) %all-to-all-start.1) | async-done | bytes 131104 | tf_op jit(solution)/shard_map/all_to_all | solution.py:47
  (162 shorter events, 33.8 us)
Async XLA Ops:
  7.2 112.8 %all-gather.3.cloned.1.call-start = ((), (), s32[]{:S(2)}) async-start(), calls=%async_computation.3 | async-start | bytes 2228224 | tf_op jit(solution)/shard_map/all_gather | solution.py:118
  26.8 291.7 %reduce-scatter.4.cloned.1.call-start = ((), (), s32[]{:S(2)}) async-start(), calls=%async_computation.4 | async-start | bytes 2228224
  29.4 95.3 %copy-start.17 = (f32[128,128]{0,1:T(8,128)}, f32[128,128]{0,1:T(8,128)S(1)}, u32[]{:S(2)}) copy-start(f32[128,128]{0,1:T(8,128)S(1)} %copy.152) | copy-start | bytes 196612
  122.6 3.8 %copy-start.28 = (f32[512,128]{0,1:T(8,128)}, f32[512,128]{0,1:T(8,128)S(1)}, u32[]{:S(2)}) copy-start(f32[512,128]{0,1:T(8,128)S(1)} %copy.96) | copy-start | bytes 786436
  123.9 3.9 %copy-start.26 = (f32[512,128]{0,1:T(8,128)}, f32[512,128]{0,1:T(8,128)S(1)}, u32[]{:S(2)}) copy-start(f32[512,128]{0,1:T(8,128)S(1)} %copy.86) | copy-start | bytes 786436
  126.4 3.6 %copy-start.19 = (f32[128,2,64]{0,2,1:T(8,128)}, f32[128,2,64]{0,2,1:T(8,128)S(1)}, u32[]{:S(2)}) copy-start(f32[128,2,64]{0,2,1:T(8,128)S(1)} %convolution_bitcast_fusion) | copy-start | bytes 196612
  126.4 3.6 %copy-start.13 = (f32[128,128]{0,1:T(8,128)S(1)}, f32[128,128]{0,1:T(8,128)}, u32[]{:S(2)}) copy-start(f32[128,128]{0,1:T(8,128)} %copy.151) | copy-start | bytes 196612
  127.7 3.4 %copy-start.24 = (f32[512,128]{0,1:T(8,128)S(1)}, f32[512,128]{0,1:T(8,128)}, u32[]{:S(2)}) copy-start(f32[512,128]{0,1:T(8,128)} %copy.91) | copy-start | bytes 786436
  131.7 19.2 %copy-start.21 = (f32[128,2,64]{0,2,1:T(8,128)}, f32[128,2,64]{0,2,1:T(8,128)S(1)}, u32[]{:S(2)}) copy-start(f32[128,2,64]{0,2,1:T(8,128)S(1)} %convolution_bitcast_fusion.1) | copy-start | bytes 196612
  132.9 13.2 %copy-start.34 = (f32[9,512]{1,0:T(8,128)S(1)}, f32[9,512]{1,0:T(8,128)}, u32[]{:S(2)}) copy-start(f32[9,512]{1,0:T(8,128)} %param.9) | copy-start | bytes 55300
  134.5 16.3 %copy-start.22 = (f32[128,2,64]{0,2,1:T(8,128)}, f32[128,2,64]{0,2,1:T(8,128)S(1)}, u32[]{:S(2)}) copy-start(f32[128,2,64]{0,2,1:T(8,128)S(1)} %convolution_bitcast_fusion.3) | copy-start | bytes 196612
  134.8 16.0 %collective-permute-start = (f32[2,1,32,512]{3,2,1,0:T(8,128)S(1)}, f32[2,1,32,512]{3,2,1,0:T(8,128)S(1)}, u32[]{:S(2)}, u32[]{:S(2)}) collective-permute-start(f32[2,1,32,512]{3,2,1,0:T(8,128)S(1)} %get-tuple-element.25), channel_id=1, source_target_pairs={{0,32},{32,64},{64,96},{96,128},{128,160},{160,192},{192,224},{224... | collective-permute-start | bytes 393224 | tf_op jit(solution)/shard_map/ppermute | solution.py:33
  136.9 13.9 %collective-permute-start.1 = (f32[2,1,32,512]{3,2,1,0:T(8,128)S(1)}, f32[2,1,32,512]{3,2,1,0:T(8,128)S(1)}, u32[]{:S(2)}, u32[]{:S(2)}) collective-permute-start(f32[2,1,32,512]{3,2,1,0:T(8,128)S(1)} %get-tuple-element.26), channel_id=1, source_target_pairs={{32,0},{64,32},{96,64},{128,96},{160,128},{192,160},{224,192},{256... | collective-permute-start | bytes 393224 | tf_op jit(solution)/shard_map/ppermute | solution.py:34
  150.9 9.0 %copy-start = (f32[4,32,512]{2,1,0:T(8,128)S(1)}, f32[4,32,512]{2,1,0:T(8,128)}, u32[]{:S(2)}) copy-start(f32[4,32,512]{2,1,0:T(8,128)} %param.8) | copy-start | bytes 786436
  150.9 5.4 %collective-permute-start.2 = (f32[2,6,1,512]{3,2,1,0:T(1,128)S(1)}, f32[2,6,1,512]{3,2,1,0:T(1,128)S(1)}, u32[]{:S(2)}, u32[]{:S(2)}) collective-permute-start(f32[2,6,1,512]{3,2,1,0:T(1,128)S(1)} %get-tuple-element.23), channel_id=1, source_target_pairs={{0,1},{1,2},{2,3},{3,4},{4,5},{5,6},{6,7},{7,8},{8,9},{9,10},{10,1... | collective-permute-start | bytes 73736 | tf_op jit(solution)/shard_map/ppermute | solution.py:33
  154.1 5.4 %collective-permute-start.3 = (f32[2,6,1,512]{3,2,1,0:T(1,128)S(1)}, f32[2,6,1,512]{3,2,1,0:T(1,128)S(1)}, u32[]{:S(2)}, u32[]{:S(2)}) collective-permute-start(f32[2,6,1,512]{3,2,1,0:T(1,128)S(1)} %get-tuple-element.24), channel_id=1, source_target_pairs={{1,0},{2,1},{3,2},{4,3},{5,4},{6,5},{7,6},{8,7},{9,8},{10,9},{11,1... | collective-permute-start | bytes 73736 | tf_op jit(solution)/shard_map/ppermute | solution.py:34
  159.9 9.9 %copy-start.20 = (f32[128,2,64]{0,2,1:T(8,128)S(1)}, f32[128,2,64]{0,2,1:T(8,128)}, u32[]{:S(2)}) copy-start(f32[128,2,64]{0,2,1:T(8,128)} %copy-done.19) | copy-start | bytes 196612
  183.7 119.1 %copy-start.2 = (f32[512,128]{0,1:T(8,128)S(1)}, f32[512,128]{0,1:T(8,128)}, u32[]{:S(2)}) copy-start(f32[512,128]{0,1:T(8,128)} %copy-done.1) | copy-start | bytes 786436
  183.7 119.1 %copy-start.8 = (f32[2,128,512]{1,2,0:T(8,128)S(1)}, f32[2,128,512]{1,2,0:T(8,128)}, u32[]{:S(2)}) copy-start(f32[2,128,512]{1,2,0:T(8,128)} %copy-done.7) | copy-start | bytes 1572868
  183.7 119.8 %copy-start.4 = (f32[512,128]{0,1:T(8,128)S(1)}, f32[512,128]{0,1:T(8,128)}, u32[]{:S(2)}) copy-start(f32[512,128]{0,1:T(8,128)} %copy-done.3) | copy-start | bytes 786436
  183.7 119.8 %copy-start.10 = (f32[2,128,512]{1,2,0:T(8,128)S(1)}, f32[2,128,512]{1,2,0:T(8,128)}, u32[]{:S(2)}) copy-start(f32[2,128,512]{1,2,0:T(8,128)} %copy-done.9) | copy-start | bytes 1572868
  183.7 120.5 %copy-start.12 = (f32[2,128,512]{1,2,0:T(8,128)S(1)}, f32[2,128,512]{1,2,0:T(8,128)}, u32[]{:S(2)}) copy-start(f32[2,128,512]{1,2,0:T(8,128)} %copy-done.11) | copy-start | bytes 1572868
  303.4 23.7 %copy-start.6 = (f32[2,128,512]{1,2,0:T(8,128)S(1)}, f32[2,128,512]{1,2,0:T(8,128)}, u32[]{:S(2)}) copy-start(f32[2,128,512]{1,2,0:T(8,128)} %copy-done.5) | copy-start | bytes 1572868
  320.4 15.2 %all-to-all-start.1 = ((f32[32,1,1024]{2,1,0:T(1,128)}), f32[32,1,1024]{2,1,0:T(1,128)S(1)}, u32[]{:S(2)}, u32[]{:S(2)}) async-start(f32[32,1,1024]{2,1,0:T(1,128)} %copy.125), calls=%async_computation.1 | async-start | bytes 262144 | tf_op jit(solution)/shard_map/all_to_all | solution.py:47
  (18 other events, 43.5 us)
Sparse Core Ops, SparseCore 0:
  26.9 93.0 all-gather.2
  183.8 134.6 reduce-scatter.3
where the time goes:
time: 344 us; the launch traced here: 343 us
  blocking collectives  136 us (40%)
  waiting for transfers between devices  116 us (34%)
  starting transfers between devices  23.4 us (7%)
  local copies, waits for them, and re-layouts  21.9 us (6%)
  matrix products  19.9 us (6%)
  between operations  16.2 us (5%)
  other arithmetic  9.35 us (3%)
    psum x1, blocking collectives, body(): tap_sum = lax.psum(tap_terms(weighted, out_padded), ('lat', 'lon'))  117 us
    all_gather x1, waiting for transfers between devices, body(): paired_all = lax.all_gather(paired_sector, 'lat', axis=0, tiled=True)  88.1 us
    all_to_all x1, blocking collectives, copy_for_each(): return lax.all_to_all(copies, axis, split_axis=0, concat_axis=0, tiled=True)  18.8 us
    unnamed x3, waiting for transfers between devices  13.6 us
    unnamed x88, local copies, waits for them, and re-layouts  13.2 us
    ppermute x2, starting transfers between devices, extended(): after = lax.ppermute(initial, axis, down)  11.3 us
  transfers between devices with their start and end apart: 7, of which 5 were waited for; matrix products, arithmetic and copies ran while one was open for 3% of the time, Pallas kernels for 0%

commit v1 on v0

--- a/solution.py
+++ b/solution.py
@@ -155,7 +155,7 @@
     grad_padded = both_padded[0]
     out_padded = both_padded[1]
     out_grad = spread_taps(weighted, grad_padded, conv_taps)
-    tap_sum = lax.psum(tap_terms(weighted, out_padded), ("lat", "lon"))
+    tap_sum = lax.psum(lax.psum(tap_terms(weighted, out_padded), "lat"), "lon")
     tap_update = tap_sum / jnp.sqrt(jnp.mean(tap_sum * tap_sum) + 1e-06)
     grad_flat = out_grad.reshape(token_count, channels)
     query_parts = []

time: 344 us -> 447 us (1.30)
  blocking collectives: 136 us -> 250 us
  waiting for transfers between devices: 116 us -> 103 us
    psum x1 -> x2, blocking collectives: 117 us -> 231 us  [body(): tap_sum = lax.psum(lax.psum(tap_terms(weighted, out_padded), 'lat'), 'lon')]
    unnamed x3, waiting for transfers between devices: 13.6 us -> 0.04 us
  transfers between devices with their start and end apart: 7 -> 7, of which waited for: 5 -> 4; matrix products, arithmetic and copies ran while one was open for 3% -> 2% of each run, Pallas kernels for 0% -> 0%
where the time goes in v1:
time: 447 us; the launch traced here: 446 us
  blocking collectives  250 us (56%)
  waiting for transfers between devices  103 us (23%)
  starting transfers between devices  26.5 us (6%)
  local copies, waits for them, and re-layouts  21.9 us (5%)
  matrix products  19.9 us (4%)
  between operations  16.2 us (4%)
  other arithmetic  9.35 us (2%)
    psum x2, blocking collectives, body(): tap_sum = lax.psum(lax.psum(tap_terms(weighted, out_padded), 'lat'), 'lon')  231 us
    all_gather x1, waiting for transfers between devices, body(): paired_all = lax.all_gather(paired_sector, 'lat', axis=0, tiled=True)  88.1 us
    all_to_all x1, blocking collectives, copy_for_each(): return lax.all_to_all(copies, axis, split_axis=0, concat_axis=0, tiled=True)  18.8 us
    unnamed x88, local copies, waits for them, and re-layouts  13.2 us
    ppermute x2, starting transfers between devices, extended(): after = lax.ppermute(initial, axis, down)  11.3 us
    all_to_all x1, starting transfers between devices, summed_on_arrival(): lax.all_to_all(cut_along(value, dim, peers), axis, 0, 0, tiled=True)  9.74 us
  transfers between devices with their start and end apart: 7, of which 4 were waited for; matrix products, arithmetic and copies ran while one was open for 2% of the time, Pallas kernels for 0%

profile of v1, /device:TPU:1, one launch (start us, length us, event | category | flops | bytes accessed | tf_op | source)
XLA Modules:
  0.0 446.2 jit_solution(890653865953472241)
XLA Ops:
  8.0 18.8 %all_to_all.10 = f32[32,1,1024]{2,1,0:T(1,128)} all-to-all(f32[32,1,1024]{2,1,0:T(1,128)S(1)} %broadcast_in_dim.10), channel_id=1, replica_groups=mesh['lat'=16,'lon'=32] {'lon'}, dimensions={0} | all-to-all | bytes 262144 | tf_op jit(solution)/shard_map/all_to_all | solution.py:19
  30.8 1.0 fusion.50
  31.8 88.1 %all-gather.3.cloned.1.call-done = f32[512,1,1024]{2,1,0:T(1,128)} async-done(((f32[32,1,1024]{2,1,0:T(1,128)}), f32[512,1,1024]{2,1,0:T(1,128)}) %all-gather.3.cloned.1.call-update) | async-done | bytes 2097168 | tf_op jit(solution)/shard_map/all_gather | solution.py:118
  120.0 2.1 copy.158
  126.7 1.0 fusion.58
  127.8 1.1 convolution_bitcast_fusion.2
  133.1 1.4 convolution_bitcast_fusion.3
  134.8 2.1 collective-permute-start
  136.9 9.2 %collective-permute-start.1 = (f32[2,1,32,512]{3,2,1,0:T(8,128)S(1)}, f32[2,1,32,512]{3,2,1,0:T(8,128)S(1)}, u32[]{:S(2)}, u32[]{:S(2)}) collective-permute-start(f32[2,1,32,512]{3,2,1,0:T(8,128)S(1)} %get-tuple-element.26), channel_id=1, source_target_pairs={{32,0},{64,32},{96,64},{128,96},{160,128},{192,160},{224,192},{256... | collective-permute-start | bytes 393224 | tf_op jit(solution)/shard_map/ppermute | solution.py:34
  146.1 4.7 %collective-permute-done = f32[2,1,32,512]{3,2,1,0:T(8,128)S(1)} collective-permute-done((f32[2,1,32,512]{3,2,1,0:T(8,128)S(1)}, f32[2,1,32,512]{3,2,1,0:T(8,128)S(1)}, u32[]{:S(2)}, u32[]{:S(2)}) %collective-permute-start) | collective-permute-done | bytes 131104 | tf_op jit(solution)/shard_map/ppermute | solution.py:33
  150.9 3.2 collective-permute-start.2
  154.1 2.1 collective-permute-start.3
  156.3 3.3 collective-permute-done.3
  160.9 1.6 copy.153
  163.3 1.6 copy.155
  165.8 1.6 copy.154
  168.2 1.6 copy.156
  170.8 1.6 fusion.38
  181.8 1.9 copy.146
  184.1 87.6 %psum.14 = f32[9,512]{1,0:T(8,128)S(1)} all-reduce(f32[9,512]{1,0:T(8,128)S(1)} %stack.47), channel_id=1, replica_groups=mesh['lat'=16,'lon'=32] {'lat'}, use_global_device_ids=true, to_apply=%region_24.25 | all-reduce | flops 4608 | bytes 36864 | tf_op jit(solution)/shard_map/psum | solution.py:158
  271.7 143.2 %psum.15 = f32[9,512]{1,0:T(8,128)S(1)} all-reduce(f32[9,512]{1,0:T(8,128)S(1)} %psum.14), channel_id=1, replica_groups=mesh['lat'=16,'lon'=32] {'lon'}, use_global_device_ids=true, to_apply=%region_25.26 | all-reduce | flops 4608 | bytes 36864 | tf_op jit(solution)/shard_map/psum | solution.py:158
  418.3 1.1 copy.147
  420.2 9.7 %all-to-all-start.1 = ((f32[32,1,1024]{2,1,0:T(1,128)}), f32[32,1,1024]{2,1,0:T(1,128)S(1)}, u32[]{:S(2)}, u32[]{:S(2)}) async-start(f32[32,1,1024]{2,1,0:T(1,128)} %copy.125), calls=%async_computation.1 | async-start | bytes 262144 | tf_op jit(solution)/shard_map/all_to_all | solution.py:47
  432.0 6.6 %all-to-all-done.1 = f32[32,1,1024]{2,1,0:T(1,128)S(1)} async-done(((f32[32,1,1024]{2,1,0:T(1,128)}), f32[32,1,1024]{2,1,0:T(1,128)S(1)}, u32[]{:S(2)}, u32[]{:S(2)}) %all-to-all-start.1) | async-done | bytes 131104 | tf_op jit(solution)/shard_map/all_to_all | solution.py:47
  (163 shorter events, 33.8 us)
Async XLA Ops:
  7.2 112.8 %all-gather.3.cloned.1.call-start = ((), (), s32[]{:S(2)}) async-start(), calls=%async_computation.3 | async-start | bytes 2228224 | tf_op jit(solution)/shard_map/all_gather | solution.py:118
  26.8 391.5 %reduce-scatter.4.cloned.1.call-start = ((), (), s32[]{:S(2)}) async-start(), calls=%async_computation.4 | async-start | bytes 2228224
  29.4 95.3 %copy-start.17 = (f32[128,128]{0,1:T(8,128)}, f32[128,128]{0,1:T(8,128)S(1)}, u32[]{:S(2)}) copy-start(f32[128,128]{0,1:T(8,128)S(1)} %copy.152) | copy-start | bytes 196612
  122.6 3.8 copy-start.28
  123.9 3.9 copy-start.26
  126.4 3.6 copy-start.19
  126.4 3.6 copy-start.13
  127.7 3.4 copy-start.24
  131.7 19.2 %copy-start.21 = (f32[128,2,64]{0,2,1:T(8,128)}, f32[128,2,64]{0,2,1:T(8,128)S(1)}, u32[]{:S(2)}) copy-start(f32[128,2,64]{0,2,1:T(8,128)S(1)} %convolution_bitcast_fusion.1) | copy-start | bytes 196612
  132.9 13.2 %copy-start.34 = (f32[9,512]{1,0:T(8,128)S(1)}, f32[9,512]{1,0:T(8,128)}, u32[]{:S(2)}) copy-start(f32[9,512]{1,0:T(8,128)} %param.9) | copy-start | bytes 55300
  134.5 16.3 %copy-start.22 = (f32[128,2,64]{0,2,1:T(8,128)}, f32[128,2,64]{0,2,1:T(8,128)S(1)}, u32[]{:S(2)}) copy-start(f32[128,2,64]{0,2,1:T(8,128)S(1)} %convolution_bitcast_fusion.3) | copy-start | bytes 196612
  134.8 16.0 %collective-permute-start = (f32[2,1,32,512]{3,2,1,0:T(8,128)S(1)}, f32[2,1,32,512]{3,2,1,0:T(8,128)S(1)}, u32[]{:S(2)}, u32[]{:S(2)}) collective-permute-start(f32[2,1,32,512]{3,2,1,0:T(8,128)S(1)} %get-tuple-element.25), channel_id=1, source_target_pairs={{0,32},{32,64},{64,96},{96,128},{128,160},{160,192},{192,224},{224... | collective-permute-start | bytes 393224 | tf_op jit(solution)/shard_map/ppermute | solution.py:33
  136.9 13.9 %collective-permute-start.1 = (f32[2,1,32,512]{3,2,1,0:T(8,128)S(1)}, f32[2,1,32,512]{3,2,1,0:T(8,128)S(1)}, u32[]{:S(2)}, u32[]{:S(2)}) collective-permute-start(f32[2,1,32,512]{3,2,1,0:T(8,128)S(1)} %get-tuple-element.26), channel_id=1, source_target_pairs={{32,0},{64,32},{96,64},{128,96},{160,128},{192,160},{224,192},{256... | collective-permute-start | bytes 393224 | tf_op jit(solution)/shard_map/ppermute | solution.py:34
  150.9 9.0 %copy-start = (f32[4,32,512]{2,1,0:T(8,128)S(1)}, f32[4,32,512]{2,1,0:T(8,128)}, u32[]{:S(2)}) copy-start(f32[4,32,512]{2,1,0:T(8,128)} %param.8) | copy-start | bytes 786436
  150.9 5.4 %collective-permute-start.2 = (f32[2,6,1,512]{3,2,1,0:T(1,128)S(1)}, f32[2,6,1,512]{3,2,1,0:T(1,128)S(1)}, u32[]{:S(2)}, u32[]{:S(2)}) collective-permute-start(f32[2,6,1,512]{3,2,1,0:T(1,128)S(1)} %get-tuple-element.23), channel_id=1, source_target_pairs={{0,1},{1,2},{2,3},{3,4},{4,5},{5,6},{6,7},{7,8},{8,9},{9,10},{10,1... | collective-permute-start | bytes 73736 | tf_op jit(solution)/shard_map/ppermute | solution.py:33
  154.1 5.4 %collective-permute-start.3 = (f32[2,6,1,512]{3,2,1,0:T(1,128)S(1)}, f32[2,6,1,512]{3,2,1,0:T(1,128)S(1)}, u32[]{:S(2)}, u32[]{:S(2)}) collective-permute-start(f32[2,6,1,512]{3,2,1,0:T(1,128)S(1)} %get-tuple-element.24), channel_id=1, source_target_pairs={{1,0},{2,1},{3,2},{4,3},{5,4},{6,5},{7,6},{8,7},{9,8},{10,9},{11,1... | collective-permute-start | bytes 73736 | tf_op jit(solution)/shard_map/ppermute | solution.py:34
  159.9 9.9 %copy-start.20 = (f32[128,2,64]{0,2,1:T(8,128)S(1)}, f32[128,2,64]{0,2,1:T(8,128)}, u32[]{:S(2)}) copy-start(f32[128,2,64]{0,2,1:T(8,128)} %copy-done.19) | copy-start | bytes 196612
  183.7 232.5 %copy-start.2 = (f32[512,128]{0,1:T(8,128)S(1)}, f32[512,128]{0,1:T(8,128)}, u32[]{:S(2)}) copy-start(f32[512,128]{0,1:T(8,128)} %copy-done.1) | copy-start | bytes 786436
  183.7 232.5 %copy-start.8 = (f32[2,128,512]{1,2,0:T(8,128)S(1)}, f32[2,128,512]{1,2,0:T(8,128)}, u32[]{:S(2)}) copy-start(f32[2,128,512]{1,2,0:T(8,128)} %copy-done.7) | copy-start | bytes 1572868
  183.7 233.2 %copy-start.4 = (f32[512,128]{0,1:T(8,128)S(1)}, f32[512,128]{0,1:T(8,128)}, u32[]{:S(2)}) copy-start(f32[512,128]{0,1:T(8,128)} %copy-done.3) | copy-start | bytes 786436
  183.7 233.2 %copy-start.10 = (f32[2,128,512]{1,2,0:T(8,128)S(1)}, f32[2,128,512]{1,2,0:T(8,128)}, u32[]{:S(2)}) copy-start(f32[2,128,512]{1,2,0:T(8,128)} %copy-done.9) | copy-start | bytes 1572868
  183.7 233.9 %copy-start.12 = (f32[2,128,512]{1,2,0:T(8,128)S(1)}, f32[2,128,512]{1,2,0:T(8,128)}, u32[]{:S(2)}) copy-start(f32[2,128,512]{1,2,0:T(8,128)} %copy-done.11) | copy-start | bytes 1572868
  416.8 13.2 %copy-start.6 = (f32[2,128,512]{1,2,0:T(8,128)S(1)}, f32[2,128,512]{1,2,0:T(8,128)}, u32[]{:S(2)}) copy-start(f32[2,128,512]{1,2,0:T(8,128)} %copy-done.5) | copy-start | bytes 1572868
  420.2 18.4 %all-to-all-start.1 = ((f32[32,1,1024]{2,1,0:T(1,128)}), f32[32,1,1024]{2,1,0:T(1,128)S(1)}, u32[]{:S(2)}, u32[]{:S(2)}) async-start(f32[32,1,1024]{2,1,0:T(1,128)} %copy.125), calls=%async_computation.1 | async-start | bytes 262144 | tf_op jit(solution)/shard_map/all_to_all | solution.py:47
  (18 other events, 43.5 us)
Sparse Core Ops, SparseCore 0:
  26.9 93.0 all-gather.2
  183.8 136.0 reduce-scatter.3
